TPU v7x, 128 devices: a whole 4x4x4 slice. The times are simulated.
128 devices in a mesh: tile: 32 (over x, z, y_lo), ell: 4 (over y_hi, core).
Axes of the slice: x: 4, y: 4 (y_hi: 2, y_lo: 2; y = y_hi * 2 + y_lo), z: 4, core: 2. Of those that a mesh axis runs over, the one named last changes fastest.
Arguments:
- spectra: float32 [55, 15360], P(None, ('tile', 'ell')), may hold values from -1 to 2
- kernel: bfloat16 [15360, 1500], P(('tile', 'ell')), may hold values from -0.046875 to 0.046875
- modes: bfloat16 [1500, 128], replicated, may hold values from -0.15625 to 0.15625
- quads: int32 [4096, 4], replicated, may hold values from 0 to 9
Outputs:
- covariance: float32 [128, 4096, 128], P('ell', 'tile')
Inputs may be any that keep to these rules, and one draw needn't show every extreme that they name: `quads`: each row (i, j, k, l) asks for the covariance between the pair of bins (i, j) and the pair (k, l).
All inputs are finite; a program needn't handle non-finite values.
Results may differ from a plain program's by a relative error of at most 0.0025.
Values may be sent and summed in bfloat16 or wider, within the bound.
A program may use at most 128 MiB of HBM per device.

v0:
```python
import math

import jax
import jax.numpy as jnp
from jax import lax
from jax.sharding import PartitionSpec as P

NB = 10
L = 15360


def sent_to_all(x, axis):
    devices = lax.axis_size(axis)
    return lax.all_to_all(jnp.broadcast_to(x[None], (devices, *x.shape)), axis, 0, 0, tiled=True)


def laid_out(blocks, dim):
    blocks = jnp.moveaxis(blocks, 0, dim)
    shape = blocks.shape
    return blocks.reshape(*shape[:dim], shape[dim] * shape[dim + 1], *shape[dim + 2 :])


def gathered_copies(x, axis, dim):
    blocks = sent_to_all(x, axis)
    return laid_out(blocks, dim)


def in_blocks(x, dim, devices):
    before, after = (x.shape[:dim], x.shape[dim + 1 :])
    return jnp.moveaxis(x.reshape(*before, devices, -1, *after), dim, 0)


def sum_at_owner(x, axis, dim):
    devices = lax.axis_size(axis)
    blocks = lax.all_to_all(in_blocks(x, dim, devices), axis, 0, 0, tiled=True)
    return jnp.sum(blocks.astype(jnp.float32), axis=0)


def pair_index(first, second):
    lower = jnp.minimum(first, second)
    upper = jnp.maximum(first, second)
    return lower * NB - lower * (lower - 1) // 2 + upper - lower


def weighted_products(columns, quad_rows, positions):
    pair_ids = jnp.concatenate(
        [
            pair_index(quad_rows[:, 0], quad_rows[:, 2]),
            pair_index(quad_rows[:, 1], quad_rows[:, 3]),
            pair_index(quad_rows[:, 0], quad_rows[:, 3]),
            pair_index(quad_rows[:, 1], quad_rows[:, 2]),
        ]
    )
    onehot = (pair_ids[:, None] == jnp.arange(columns.shape[0], dtype=jnp.int32)[None, :]).astype(
        jnp.float32
    )
    picked = jnp.dot(
        onehot, columns, precision=lax.Precision.HIGHEST, preferred_element_type=jnp.float32
    )
    picked = picked.reshape(4, quad_rows.shape[0], columns.shape[1])
    weight = (2 * positions + 5).astype(jnp.float32) * (0.5 / math.sqrt(L))
    return weight[None, :] * (picked[0] * picked[1] + picked[2] * picked[3])


def tile_positions(tile_count, ell_count, ell_id, local_rows):
    offsets = jnp.arange(tile_count * local_rows, dtype=jnp.int32)
    return (offsets // local_rows * ell_count + ell_id) * local_rows + offsets % local_rows


def tile_products(spectra, quads, ell_id, tile_id):
    tile_count = lax.axis_size("tile")
    ell_count = lax.axis_size("ell")
    local_rows = spectra.shape[1]
    per_tile = quads.shape[0] // tile_count
    own_quads = lax.dynamic_slice_in_dim(quads, tile_id * per_tile, per_tile, 0)
    columns = gathered_copies(spectra, "tile", 1)
    return weighted_products(
        columns, own_quads, tile_positions(tile_count, ell_count, ell_id, local_rows)
    )


def contract(compressed, products, count):
    quad_count = products.shape[0]
    row_count = products.shape[1]
    width = compressed.shape[1]
    by_row = products.T

    def step(index, total):
        block = lax.dynamic_slice_in_dim(by_row, index * 4, 4, 1)
        scaled = (
            (block[:, :, None] * compressed[:, None, :])
            .astype(jnp.bfloat16)
            .reshape(row_count, 4 * width)
        )
        part = lax.dot_general(
            compressed, scaled, (((0,), (0,)), ((), ())), preferred_element_type=jnp.float32
        )
        part = part.reshape(count, 4, width)
        return lax.dynamic_update_slice_in_dim(total, part, index * 4, 1)

    initial = jnp.zeros((count, quad_count, width), jnp.float32)
    return lax.fori_loop(0, quad_count // 4, step, initial)


def body(spectra, kernel, modes, quads):
    tile_id = lax.axis_index("tile")
    ell_id = lax.axis_index("ell")
    ell_count = lax.axis_size("ell")
    compressed = jnp.dot(kernel, modes, preferred_element_type=jnp.float32).astype(jnp.bfloat16)
    products = tile_products(spectra, quads, ell_id, tile_id)
    gathered = gathered_copies(compressed, "tile", 0)
    share = modes.shape[1] // ell_count
    return sum_at_owner(
        contract(gathered, products, share * lax.axis_size("ell")).astype(jnp.bfloat16), "ell", 0
    )


def solution(mesh):
    return jax.shard_map(
        body,
        mesh=mesh,
        in_specs=(P(None, ("tile", "ell")), P(("tile", "ell"), None), P(), P()),
        out_specs=P("ell", "tile", None),
        check_vma=False,
    )
```

profile of v0, /device:TPU:1, one launch (start us, length us, event | category | flops | bytes accessed | tf_op | source)
XLA Modules:
  0.0 391.7 jit_solution(2940960912924702399)
XLA Ops:
  0.0 1.8 broadcast_in_dim.9
  1.8 9.7 %all-to-all-start = ((f32[32,55,120]{2,1,0:T(8,128)}), f32[32,55,120]{2,1,0:T(8,128)S(1)}, u32[]{:S(2)}, u32[]{:S(2)}) async-start(f32[32,55,120]{2,1,0:T(8,128)} %broadcast_in_dim.9), calls=%async_computation | async-start | bytes 1835008 | tf_op jit(solution)/shard_map/all_to_all | solution.py:14
  13.5 12.7 %all-to-all-done = f32[32,55,120]{2,1,0:T(8,128)S(1)} async-done(((f32[32,55,120]{2,1,0:T(8,128)}), f32[32,55,120]{2,1,0:T(8,128)S(1)}, u32[]{:S(2)}, u32[]{:S(2)}) %all-to-all-start) | async-done | bytes 844832 | tf_op jit(solution)/shard_map/all_to_all | solution.py:14
  27.3 4.3 %all-to-all-start.1 = ((bf16[32,120,128]{2,1,0:T(8,128)(2,1)}), bf16[32,120,128]{2,1,0:T(8,128)(2,1)S(1)}, u32[]{:S(2)}, u32[]{:S(2)}) async-start(bf16[32,120,128]{2,1,0:T(8,128)(2,1)} %broadcast_in_dim.10), calls=%async_computation.1 | async-start | bytes 1966080 | tf_op jit(solution)/shard_map/all_to_all | solution.py:14
  32.4 3.3 fusion.6
  35.7 1.7 fusion.5
  37.4 9.2 %all-to-all-done.1 = bf16[32,120,128]{2,1,0:T(8,128)(2,1)S(1)} async-done(((bf16[32,120,128]{2,1,0:T(8,128)(2,1)}), bf16[32,120,128]{2,1,0:T(8,128)(2,1)S(1)}, u32[]{:S(2)}, u32[]{:S(2)}) %all-to-all-start.1) | async-done | bytes 983072 | tf_op jit(solution)/shard_map/all_to_all | solution.py:14
  46.6 3.0 broadcast_in_dim.8.clone
  49.6 284.5 %while.13 = (s32[]{:T(128)}, bf16[128,128,128]{2,1,0:T(8,128)(2,1)}, f32[3840,128]{0,1:T(8,128)}, bf16[32,120,128]{2,1,0:T(8,128)(2,1)S(1)}, bf16[3840,128]{1,0:...) while((s32[]{:T(128)}, bf16[128,128,128]{2,1,0:T(8,128)(2,1)}, f32[3840,128]{0,1:T(8,128)}, ...), condition=%wide.region_1.2_spmd, body=%wide.region_0.1_spmd.sunk | while | flops 507740160 | bytes 14725267 | solution.py:102
  51.3 5.0 %multiply_convert_fusion.2 = bf16[3840,4,128]{2,1,0:T(4,128)(2,1)S(1)} fusion(f32[3840,128]{1,0:T(8,128)S(1)} %bitcast_convert_fusion.2, f32[3840,4]{1,0:T(8,128)S(1)} %copy.24), kind=kLoop, calls=%fused_computation.clone.1 | loop fusion | flops 3932160 | bytes 5959680 | tf_op jit(solution)/shard_map/while/body/eval_jaxpr/convert_element_type | solution.py:92
  56.3 1.3 fusion.40
  60.2 5.0 %multiply_convert_fusion.2 = bf16[3840,4,128]{2,1,0:T(4,128)(2,1)S(1)} fusion(f32[3840,128]{1,0:T(8,128)S(1)} %bitcast_convert_fusion.2, f32[3840,4]{1,0:T(8,128)S(1)} %copy.24), kind=kLoop, calls=%fused_computation.clone.1 | loop fusion | flops 3932160 | bytes 5959680 | tf_op jit(solution)/shard_map/while/body/eval_jaxpr/convert_element_type | solution.py:92
  69.1 5.0 %multiply_convert_fusion.2 = bf16[3840,4,128]{2,1,0:T(4,128)(2,1)S(1)} fusion(f32[3840,128]{1,0:T(8,128)S(1)} %bitcast_convert_fusion.2, f32[3840,4]{1,0:T(8,128)S(1)} %copy.24), kind=kLoop, calls=%fused_computation.clone.1 | loop fusion | flops 3932160 | bytes 5959680 | tf_op jit(solution)/shard_map/while/body/eval_jaxpr/convert_element_type | solution.py:92
  74.1 1.3 fusion.40
  78.0 5.0 %multiply_convert_fusion.2 = bf16[3840,4,128]{2,1,0:T(4,128)(2,1)S(1)} fusion(f32[3840,128]{1,0:T(8,128)S(1)} %bitcast_convert_fusion.2, f32[3840,4]{1,0:T(8,128)S(1)} %copy.24), kind=kLoop, calls=%fused_computation.clone.1 | loop fusion | flops 3932160 | bytes 5959680 | tf_op jit(solution)/shard_map/while/body/eval_jaxpr/convert_element_type | solution.py:92
  86.9 5.0 %multiply_convert_fusion.2 = bf16[3840,4,128]{2,1,0:T(4,128)(2,1)S(1)} fusion(f32[3840,128]{1,0:T(8,128)S(1)} %bitcast_convert_fusion.2, f32[3840,4]{1,0:T(8,128)S(1)} %copy.24), kind=kLoop, calls=%fused_computation.clone.1 | loop fusion | flops 3932160 | bytes 5959680 | tf_op jit(solution)/shard_map/while/body/eval_jaxpr/convert_element_type | solution.py:92
  91.9 1.3 fusion.40
  95.8 5.0 %multiply_convert_fusion.2 = bf16[3840,4,128]{2,1,0:T(4,128)(2,1)S(1)} fusion(f32[3840,128]{1,0:T(8,128)S(1)} %bitcast_convert_fusion.2, f32[3840,4]{1,0:T(8,128)S(1)} %copy.24), kind=kLoop, calls=%fused_computation.clone.1 | loop fusion | flops 3932160 | bytes 5959680 | tf_op jit(solution)/shard_map/while/body/eval_jaxpr/convert_element_type | solution.py:92
  104.6 5.0 %multiply_convert_fusion.2 = bf16[3840,4,128]{2,1,0:T(4,128)(2,1)S(1)} fusion(f32[3840,128]{1,0:T(8,128)S(1)} %bitcast_convert_fusion.2, f32[3840,4]{1,0:T(8,128)S(1)} %copy.24), kind=kLoop, calls=%fused_computation.clone.1 | loop fusion | flops 3932160 | bytes 5959680 | tf_op jit(solution)/shard_map/while/body/eval_jaxpr/convert_element_type | solution.py:92
  113.5 5.0 %multiply_convert_fusion.2 = bf16[3840,4,128]{2,1,0:T(4,128)(2,1)S(1)} fusion(f32[3840,128]{1,0:T(8,128)S(1)} %bitcast_convert_fusion.2, f32[3840,4]{1,0:T(8,128)S(1)} %copy.24), kind=kLoop, calls=%fused_computation.clone.1 | loop fusion | flops 3932160 | bytes 5959680 | tf_op jit(solution)/shard_map/while/body/eval_jaxpr/convert_element_type | solution.py:92
  122.4 5.0 %multiply_convert_fusion.2 = bf16[3840,4,128]{2,1,0:T(4,128)(2,1)S(1)} fusion(f32[3840,128]{1,0:T(8,128)S(1)} %bitcast_convert_fusion.2, f32[3840,4]{1,0:T(8,128)S(1)} %copy.24), kind=kLoop, calls=%fused_computation.clone.1 | loop fusion | flops 3932160 | bytes 5959680 | tf_op jit(solution)/shard_map/while/body/eval_jaxpr/convert_element_type | solution.py:92
  131.3 5.0 %multiply_convert_fusion.2 = bf16[3840,4,128]{2,1,0:T(4,128)(2,1)S(1)} fusion(f32[3840,128]{1,0:T(8,128)S(1)} %bitcast_convert_fusion.2, f32[3840,4]{1,0:T(8,128)S(1)} %copy.24), kind=kLoop, calls=%fused_computation.clone.1 | loop fusion | flops 3932160 | bytes 5959680 | tf_op jit(solution)/shard_map/while/body/eval_jaxpr/convert_element_type | solution.py:92
  140.3 5.0 %multiply_convert_fusion.2 = bf16[3840,4,128]{2,1,0:T(4,128)(2,1)S(1)} fusion(f32[3840,128]{1,0:T(8,128)S(1)} %bitcast_convert_fusion.2, f32[3840,4]{1,0:T(8,128)S(1)} %copy.24), kind=kLoop, calls=%fused_computation.clone.1 | loop fusion | flops 3932160 | bytes 5959680 | tf_op jit(solution)/shard_map/while/body/eval_jaxpr/convert_element_type | solution.py:92
  149.2 5.0 %multiply_convert_fusion.2 = bf16[3840,4,128]{2,1,0:T(4,128)(2,1)S(1)} fusion(f32[3840,128]{1,0:T(8,128)S(1)} %bitcast_convert_fusion.2, f32[3840,4]{1,0:T(8,128)S(1)} %copy.24), kind=kLoop, calls=%fused_computation.clone.1 | loop fusion | flops 3932160 | bytes 5959680 | tf_op jit(solution)/shard_map/while/body/eval_jaxpr/convert_element_type | solution.py:92
  154.2 1.3 fusion.40
  158.1 5.0 %multiply_convert_fusion.2 = bf16[3840,4,128]{2,1,0:T(4,128)(2,1)S(1)} fusion(f32[3840,128]{1,0:T(8,128)S(1)} %bitcast_convert_fusion.2, f32[3840,4]{1,0:T(8,128)S(1)} %copy.24), kind=kLoop, calls=%fused_computation.clone.1 | loop fusion | flops 3932160 | bytes 5959680 | tf_op jit(solution)/shard_map/while/body/eval_jaxpr/convert_element_type | solution.py:92
  167.0 5.0 %multiply_convert_fusion.2 = bf16[3840,4,128]{2,1,0:T(4,128)(2,1)S(1)} fusion(f32[3840,128]{1,0:T(8,128)S(1)} %bitcast_convert_fusion.2, f32[3840,4]{1,0:T(8,128)S(1)} %copy.24), kind=kLoop, calls=%fused_computation.clone.1 | loop fusion | flops 3932160 | bytes 5959680 | tf_op jit(solution)/shard_map/while/body/eval_jaxpr/convert_element_type | solution.py:92
  175.8 5.0 %multiply_convert_fusion.2 = bf16[3840,4,128]{2,1,0:T(4,128)(2,1)S(1)} fusion(f32[3840,128]{1,0:T(8,128)S(1)} %bitcast_convert_fusion.2, f32[3840,4]{1,0:T(8,128)S(1)} %copy.24), kind=kLoop, calls=%fused_computation.clone.1 | loop fusion | flops 3932160 | bytes 5959680 | tf_op jit(solution)/shard_map/while/body/eval_jaxpr/convert_element_type | solution.py:92
  184.7 5.0 %multiply_convert_fusion.2 = bf16[3840,4,128]{2,1,0:T(4,128)(2,1)S(1)} fusion(f32[3840,128]{1,0:T(8,128)S(1)} %bitcast_convert_fusion.2, f32[3840,4]{1,0:T(8,128)S(1)} %copy.24), kind=kLoop, calls=%fused_computation.clone.1 | loop fusion | flops 3932160 | bytes 5959680 | tf_op jit(solution)/shard_map/while/body/eval_jaxpr/convert_element_type | solution.py:92
  193.6 5.0 %multiply_convert_fusion.2 = bf16[3840,4,128]{2,1,0:T(4,128)(2,1)S(1)} fusion(f32[3840,128]{1,0:T(8,128)S(1)} %bitcast_convert_fusion.2, f32[3840,4]{1,0:T(8,128)S(1)} %copy.24), kind=kLoop, calls=%fused_computation.clone.1 | loop fusion | flops 3932160 | bytes 5959680 | tf_op jit(solution)/shard_map/while/body/eval_jaxpr/convert_element_type | solution.py:92
  202.5 5.0 %multiply_convert_fusion.2 = bf16[3840,4,128]{2,1,0:T(4,128)(2,1)S(1)} fusion(f32[3840,128]{1,0:T(8,128)S(1)} %bitcast_convert_fusion.2, f32[3840,4]{1,0:T(8,128)S(1)} %copy.24), kind=kLoop, calls=%fused_computation.clone.1 | loop fusion | flops 3932160 | bytes 5959680 | tf_op jit(solution)/shard_map/while/body/eval_jaxpr/convert_element_type | solution.py:92
  211.4 5.0 %multiply_convert_fusion.2 = bf16[3840,4,128]{2,1,0:T(4,128)(2,1)S(1)} fusion(f32[3840,128]{1,0:T(8,128)S(1)} %bitcast_convert_fusion.2, f32[3840,4]{1,0:T(8,128)S(1)} %copy.24), kind=kLoop, calls=%fused_computation.clone.1 | loop fusion | flops 3932160 | bytes 5959680 | tf_op jit(solution)/shard_map/while/body/eval_jaxpr/convert_element_type | solution.py:92
  220.3 5.0 %multiply_convert_fusion.2 = bf16[3840,4,128]{2,1,0:T(4,128)(2,1)S(1)} fusion(f32[3840,128]{1,0:T(8,128)S(1)} %bitcast_convert_fusion.2, f32[3840,4]{1,0:T(8,128)S(1)} %copy.24), kind=kLoop, calls=%fused_computation.clone.1 | loop fusion | flops 3932160 | bytes 5959680 | tf_op jit(solution)/shard_map/while/body/eval_jaxpr/convert_element_type | solution.py:92
  229.2 5.0 %multiply_convert_fusion.2 = bf16[3840,4,128]{2,1,0:T(4,128)(2,1)S(1)} fusion(f32[3840,128]{1,0:T(8,128)S(1)} %bitcast_convert_fusion.2, f32[3840,4]{1,0:T(8,128)S(1)} %copy.24), kind=kLoop, calls=%fused_computation.clone.1 | loop fusion | flops 3932160 | bytes 5959680 | tf_op jit(solution)/shard_map/while/body/eval_jaxpr/convert_element_type | solution.py:92
  238.1 5.0 %multiply_convert_fusion.2 = bf16[3840,4,128]{2,1,0:T(4,128)(2,1)S(1)} fusion(f32[3840,128]{1,0:T(8,128)S(1)} %bitcast_convert_fusion.2, f32[3840,4]{1,0:T(8,128)S(1)} %copy.24), kind=kLoop, calls=%fused_computation.clone.1 | loop fusion | flops 3932160 | bytes 5959680 | tf_op jit(solution)/shard_map/while/body/eval_jaxpr/convert_element_type | solution.py:92
  246.9 5.0 %multiply_convert_fusion.2 = bf16[3840,4,128]{2,1,0:T(4,128)(2,1)S(1)} fusion(f32[3840,128]{1,0:T(8,128)S(1)} %bitcast_convert_fusion.2, f32[3840,4]{1,0:T(8,128)S(1)} %copy.24), kind=kLoop, calls=%fused_computation.clone.1 | loop fusion | flops 3932160 | bytes 5959680 | tf_op jit(solution)/shard_map/while/body/eval_jaxpr/convert_element_type | solution.py:92
  255.8 5.0 %multiply_convert_fusion.2 = bf16[3840,4,128]{2,1,0:T(4,128)(2,1)S(1)} fusion(f32[3840,128]{1,0:T(8,128)S(1)} %bitcast_convert_fusion.2, f32[3840,4]{1,0:T(8,128)S(1)} %copy.24), kind=kLoop, calls=%fused_computation.clone.1 | loop fusion | flops 3932160 | bytes 5959680 | tf_op jit(solution)/shard_map/while/body/eval_jaxpr/convert_element_type | solution.py:92
  260.8 1.3 fusion.40
  264.7 5.0 %multiply_convert_fusion.2 = bf16[3840,4,128]{2,1,0:T(4,128)(2,1)S(1)} fusion(f32[3840,128]{1,0:T(8,128)S(1)} %bitcast_convert_fusion.2, f32[3840,4]{1,0:T(8,128)S(1)} %copy.24), kind=kLoop, calls=%fused_computation.clone.1 | loop fusion | flops 3932160 | bytes 5959680 | tf_op jit(solution)/shard_map/while/body/eval_jaxpr/convert_element_type | solution.py:92
  273.6 5.0 %multiply_convert_fusion.2 = bf16[3840,4,128]{2,1,0:T(4,128)(2,1)S(1)} fusion(f32[3840,128]{1,0:T(8,128)S(1)} %bitcast_convert_fusion.2, f32[3840,4]{1,0:T(8,128)S(1)} %copy.24), kind=kLoop, calls=%fused_computation.clone.1 | loop fusion | flops 3932160 | bytes 5959680 | tf_op jit(solution)/shard_map/while/body/eval_jaxpr/convert_element_type | solution.py:92
  282.5 5.0 %multiply_convert_fusion.2 = bf16[3840,4,128]{2,1,0:T(4,128)(2,1)S(1)} fusion(f32[3840,128]{1,0:T(8,128)S(1)} %bitcast_convert_fusion.2, f32[3840,4]{1,0:T(8,128)S(1)} %copy.24), kind=kLoop, calls=%fused_computation.clone.1 | loop fusion | flops 3932160 | bytes 5959680 | tf_op jit(solution)/shard_map/while/body/eval_jaxpr/convert_element_type | solution.py:92
  291.4 5.0 %multiply_convert_fusion.2 = bf16[3840,4,128]{2,1,0:T(4,128)(2,1)S(1)} fusion(f32[3840,128]{1,0:T(8,128)S(1)} %bitcast_convert_fusion.2, f32[3840,4]{1,0:T(8,128)S(1)} %copy.24), kind=kLoop, calls=%fused_computation.clone.1 | loop fusion | flops 3932160 | bytes 5959680 | tf_op jit(solution)/shard_map/while/body/eval_jaxpr/convert_element_type | solution.py:92
  300.3 5.0 %multiply_convert_fusion.2 = bf16[3840,4,128]{2,1,0:T(4,128)(2,1)S(1)} fusion(f32[3840,128]{1,0:T(8,128)S(1)} %bitcast_convert_fusion.2, f32[3840,4]{1,0:T(8,128)S(1)} %copy.24), kind=kLoop, calls=%fused_computation.clone.1 | loop fusion | flops 3932160 | bytes 5959680 | tf_op jit(solution)/shard_map/while/body/eval_jaxpr/convert_element_type | solution.py:92
  309.2 5.0 %multiply_convert_fusion.2 = bf16[3840,4,128]{2,1,0:T(4,128)(2,1)S(1)} fusion(f32[3840,128]{1,0:T(8,128)S(1)} %bitcast_convert_fusion.2, f32[3840,4]{1,0:T(8,128)S(1)} %copy.24), kind=kLoop, calls=%fused_computation.clone.1 | loop fusion | flops 3932160 | bytes 5959680 | tf_op jit(solution)/shard_map/while/body/eval_jaxpr/convert_element_type | solution.py:92
  318.0 5.0 %multiply_convert_fusion.2 = bf16[3840,4,128]{2,1,0:T(4,128)(2,1)S(1)} fusion(f32[3840,128]{1,0:T(8,128)S(1)} %bitcast_convert_fusion.2, f32[3840,4]{1,0:T(8,128)S(1)} %copy.24), kind=kLoop, calls=%fused_computation.clone.1 | loop fusion | flops 3932160 | bytes 5959680 | tf_op jit(solution)/shard_map/while/body/eval_jaxpr/convert_element_type | solution.py:92
  326.9 5.0 %multiply_convert_fusion.2 = bf16[3840,4,128]{2,1,0:T(4,128)(2,1)S(1)} fusion(f32[3840,128]{1,0:T(8,128)S(1)} %bitcast_convert_fusion.2, f32[3840,4]{1,0:T(8,128)S(1)} %copy.24), kind=kLoop, calls=%fused_computation.clone.1 | loop fusion | flops 3932160 | bytes 5959680 | tf_op jit(solution)/shard_map/while/body/eval_jaxpr/convert_element_type | solution.py:92
  334.1 55.5 %all_to_all.15 = bf16[4,32,128,128]{3,2,1,0:T(8,128)(2,1)S(1)} all-to-all(bf16[4,32,128,128]{3,2,1,0:T(8,128)(2,1)} %bitcast.89), channel_id=1, replica_groups=mesh['tile'=32,'ell'=4] {'ell'}, dimensions={0} | all-to-all | bytes 8388608 | tf_op jit(solution)/shard_map/all_to_all | solution.py:35
  389.6 2.1 convert_reduce_fusion
  (197 shorter events, 121.4 us)
Async XLA Ops:
  0.0 12.3 %copy-start = (bf16[1500,128]{1,0:T(8,128)(2,1)S(1)}, bf16[1500,128]{1,0:T(8,128)(2,1)}, u32[]{:S(2)}) copy-start(bf16[1500,128]{1,0:T(8,128)(2,1)} %param.8) | copy-start | bytes 1152004
  1.8 24.4 %all-to-all-start = ((f32[32,55,120]{2,1,0:T(8,128)}), f32[32,55,120]{2,1,0:T(8,128)S(1)}, u32[]{:S(2)}, u32[]{:S(2)}) async-start(f32[32,55,120]{2,1,0:T(8,128)} %broadcast_in_dim.9), calls=%async_computation | async-start | bytes 1835008 | tf_op jit(solution)/shard_map/all_to_all | solution.py:14
  27.3 19.3 %all-to-all-start.1 = ((bf16[32,120,128]{2,1,0:T(8,128)(2,1)}), bf16[32,120,128]{2,1,0:T(8,128)(2,1)S(1)}, u32[]{:S(2)}, u32[]{:S(2)}) async-start(bf16[32,120,128]{2,1,0:T(8,128)(2,1)} %broadcast_in_dim.10), calls=%async_computation.1 | async-start | bytes 1966080 | tf_op jit(solution)/shard_map/all_to_all | solution.py:14
where the time goes:
time: 393 us; the launch traced here: 392 us
  other arithmetic  169 us (43%)
  local copies, waits for them, and re-layouts  84 us (21%)
  blocking collectives  55.5 us (14%)
  matrix products  45.6 us (12%)
  waiting for transfers between devices  21.9 us (6%)
  starting transfers between devices  14 us (4%)
    convert_element_type x32, other arithmetic, step(): scaled = (block[:, :, None] * compressed[:, None, :]).astype(jnp.bfloat16...  159 us
    all_to_all x1, blocking collectives, sum_at_owner(): blocks = lax.all_to_all(in_blocks(x, dim, devices), axis, 0, 0, tiled=True)  55.5 us
    dynamic_slice x64, local copies, waits for them, and re-layouts, step(): block = lax.dynamic_slice_in_dim(by_row, index * 4, 4, 1)  48.5 us
    dot_general x32, matrix products, step(): lax.dot_general(compressed, scaled, (((0,), (0,)), ((), ())), preferred_e...  41.1 us
    dynamic_update_slice x64, local copies, waits for them, and re-layouts, step(): return lax.dynamic_update_slice_in_dim(total, part, index * 4, 1)  28.1 us
    all_to_all x2, waiting for transfers between devices, sent_to_all(): lax.all_to_all(jnp.broadcast_to(x[None], (devices, *x.shape)), axis, 0, 0...  21.9 us
    all_to_all x2, starting transfers between devices, sent_to_all(): lax.all_to_all(jnp.broadcast_to(x[None], (devices, *x.shape)), axis, 0, 0...  14 us
  transfers between devices with their start and end apart: 2, of which 2 were waited for; matrix products, arithmetic and copies ran while one was open for 2% of the time, Pallas kernels for 0%

commit v1 on v0

v1 whole, which is shorter than its diff:
```python
import functools
import math

import jax
import jax.numpy as jnp
from jax import lax
from jax.experimental import pallas as pl
from jax.experimental.pallas import tpu as pltpu
from jax.sharding import PartitionSpec as P

NB = 10
L = 15360
ROWS = 128
SROWS = 64
GROUP = 8
BLOCKS = 64
F32 = jnp.float32
BF16 = jnp.bfloat16


def pair_index(first, second):
    lower = jnp.minimum(first, second)
    upper = jnp.maximum(first, second)
    return lower * NB - lower * (lower - 1) // 2 + upper - lower


def contraction(pairs, c_ref, s_ref, mine, theirs, left, right, lhs, wide, prods, acc):
    ell = lax.axis_index("ell")
    half, core = ell // 2, ell % 2
    lane = lax.broadcasted_iota(jnp.int32, (ROWS, 128), 1)
    sublane = lax.broadcasted_iota(jnp.int32, (GROUP, 128), 0)
    lane8 = lax.broadcasted_iota(jnp.int32, (GROUP, 128), 1)
    scale = 0.5 / math.sqrt(L)

    def block(group, j):
        return lax.rem(group * GROUP + j, BLOCKS)

    def weights(group):
        base = jnp.zeros((GROUP, 128), jnp.int32)
        for j in range(GROUP):
            base = jnp.where(sublane == j, (2 * block(group, j) + core) * 120, base)
        return (2 * (base + lane8) + 5).astype(F32) * scale

    def widen(group):
        for j in range(GROUP):
            wide[j * SROWS : (j + 1) * SROWS, :] = s_ref[block(group, j)].astype(F32)

    def product(q, weight):
        ik, jl, il, jk = (
            wide[pl.ds(pairs[k, q], GROUP, stride=SROWS), :] for k in range(4)
        )
        prods[pl.ds(q, GROUP, stride=128), :] = weight * (ik * jl + il * jk)

    def finish(slot):
        for j in range(GROUP):
            lhs[slot, :, j * ROWS : (j + 1) * ROWS] = prods[j * 128 : (j + 1) * 128, :].astype(BF16)

    def pattern(slot, group, j, i):
        x = c_ref[block(group, j)].astype(F32)
        rows = slice(j * ROWS, (j + 1) * ROWS)
        if i < 8:
            at = half * 64 + lax.rem(core * 32 + 8 * i, 64) + lane // 16
            left[slot, i, rows, :] = jnp.take_along_axis(x, at, axis=1).astype(BF16)
        else:
            at = 16 * (i - 8) + lane % 16
            right[slot, i - 8, rows, :] = jnp.take_along_axis(x, at, axis=1).astype(BF16)

    every = [(j, i) for j in range(GROUP) for i in range(16)]

    widen(0)
    first_weight = weights(0)
    lax.fori_loop(0, 128, lambda q, _: product(q, first_weight), None)
    finish(0)
    for j, i in every:
        pattern(0, 0, j, i)
    acc[...] = jnp.zeros_like(acc)

    def two(step, _):
        for slot in range(2):
            following = step * 2 + slot + 1
            widen(following)
            weight = weights(following)
            for n in range(32):
                for j, i in every[4 * n : 4 * n + 4]:
                    pattern(1 - slot, following, j, i)
                for q in range(4 * n, 4 * n + 4):
                    product(q, weight)
                rhs = jnp.concatenate(
                    [left[slot, m // 8] * right[slot, m % 8] for m in (2 * n, 2 * n + 1)], axis=1
                )
                acc[:, n * 256 : (n + 1) * 256] += jnp.dot(
                    lhs[slot], rhs, preferred_element_type=F32
                )
            finish(1 - slot)

    lax.fori_loop(0, BLOCKS // GROUP // 2, two, None)
    mine[...] = acc[:, :4096]
    theirs[...] = acc[:, 4096:].astype(BF16)


def contract(pairs, c_all, s_all):
    vmem = pl.BlockSpec(memory_space=pltpu.VMEM)
    return pl.pallas_call(
        contraction,
        out_shape=(
            jax.ShapeDtypeStruct((128, 4096), F32),
            jax.ShapeDtypeStruct((128, 4096), BF16),
        ),
        in_specs=[pl.BlockSpec(memory_space=pltpu.SMEM), vmem, vmem],
        out_specs=(vmem, vmem),
        scratch_shapes=[
            pltpu.VMEM((2, 8, GROUP * ROWS, 128), BF16),
            pltpu.VMEM((2, 8, GROUP * ROWS, 128), BF16),
            pltpu.VMEM((2, 128, GROUP * ROWS), BF16),
            pltpu.VMEM((GROUP * SROWS, 128), F32),
            pltpu.VMEM((GROUP * 128, 128), F32),
            pltpu.VMEM((128, 8192), F32),
        ],
        compiler_params=pltpu.CompilerParams(vmem_limit_bytes=60 * 2**20),
    )(pairs, c_all, s_all)


def spread(mine, theirs, out):
    lane = lax.broadcasted_iota(jnp.int32, (128, 128), 1)
    cols = [slice(j * 128, (j + 1) * 128) for j in range(8)]
    v = [mine[:, c] + theirs[:, c].astype(F32) for c in cols]
    for k in (1, 2, 4):
        low = (lane // 16) & k == 0
        for m in range(8):
            if m & k == 0:
                a, b = v[m], v[m + k]
                v[m] = jnp.where(low, a, pltpu.roll(b, 16 * k, 1))
                v[m + k] = jnp.where(low, pltpu.roll(a, 128 - 16 * k, 1), b)
    for m in range(8):
        out[m] = v[m]


def combine(mine, theirs):
    return pl.pallas_call(
        spread,
        out_shape=jax.ShapeDtypeStruct((32, 128, 128), F32),
        grid=(4,),
        in_specs=[pl.BlockSpec((128, 1024), lambda i: (0, i))] * 2,
        out_specs=pl.BlockSpec((8, 128, 128), lambda i: (i, 0, 0)),
    )(mine, theirs)


def body(spectra, kernel, modes, quads):
    tile_count, ell_count = lax.axis_size("tile"), lax.axis_size("ell")
    compressed = jnp.dot(kernel, modes, preferred_element_type=F32).astype(BF16)
    local = jnp.concatenate(
        [
            jnp.pad(compressed, ((0, ROWS - 120), (0, 0))),
            jnp.pad(spectra.astype(BF16), ((0, SROWS - 55), (0, ROWS - 120))),
        ]
    )
    groups = [
        [4 * t + 2 * h + core for t in range(tile_count) for h in range(ell_count // 2)]
        for core in range(2)
    ]
    every = lax.all_gather(local, ("tile", "ell"), axis_index_groups=groups)
    own = lax.dynamic_slice_in_dim(quads, lax.axis_index("tile") * 128, 128, 0).T
    i, j, k, l = own[0], own[1], own[2], own[3]
    pairs = jnp.stack([pair_index(i, k), pair_index(j, l), pair_index(i, l), pair_index(j, k)])
    mine, theirs = contract(pairs, every[:, :ROWS], every[:, ROWS:])
    theirs = lax.ppermute(theirs, "ell", [(0, 1), (1, 0), (2, 3), (3, 2)])
    return combine(mine, theirs)


def solution(mesh):
    return jax.shard_map(
        body,
        mesh=mesh,
        in_specs=(P(None, ("tile", "ell")), P(("tile", "ell"), None), P(), P()),
        out_specs=P("ell", "tile", None),
        check_vma=False,
    )
```

time: 393 us -> 423 us (1.076)
  waiting for transfers between devices: 21.9 us -> 292 us
  other arithmetic: 169 us -> 2.04 us
  local copies, waits for them, and re-layouts: 84 us -> 7.33 us
  Pallas kernels: 0 us -> 58.8 us
  blocking collectives: 55.5 us -> 0 us
  matrix products: 45.6 us -> 1.23 us
  starting transfers between devices: 14 us -> 47.2 us
  between operations: 0.07 us -> 13.4 us
    all_gather x0 -> x1, waiting for transfers between devices: none -> 290 us  [body(): every = lax.all_gather(local, ('tile', 'ell'), axis_index_groups=groups)]
    convert_element_type x64 -> x1, other arithmetic: 165 us -> 0.8 us  [body(): spectra.astype(BF16)]
    pallas_call x0 -> x2, Pallas kernels: none -> 58.8 us  [the longest x1 54 us: contract(): pl.pallas_call(contraction, out_shape=(jax.ShapeDtypeStruct((128, 4096),...]
    all_to_all x1 -> x0, blocking collectives: 55.5 us -> none  [sum_at_owner(): blocks = lax.all_to_all(in_blocks(x, dim, devices), axis, 0, 0, tiled=True)]
    dynamic_slice x65 -> x0, local copies, waits for them, and re-layouts: 49.2 us -> none  [the longest x64 48.5 us: step(): block = lax.dynamic_slice_in_dim(by_row, index * 4, 4, 1)]
    ppermute x0 -> x1, starting transfers between devices: none -> 47.2 us  [body(): theirs = lax.ppermute(theirs, 'ell', [(0, 1), (1, 0), (2, 3), (3, 2)])]
    dot_general x34 -> x1, matrix products: 45.6 us -> 1.23 us  [body(): compressed = jnp.dot(kernel, modes, preferred_element_type=F32).astype(BF16)]
    dynamic_update_slice x64 -> x0, local copies, waits for them, and re-layouts: 28.1 us -> none  [step(): return lax.dynamic_update_slice_in_dim(total, part, index * 4, 1)]
  transfers between devices with their start and end apart: 2 -> 2, of which waited for: 2 -> 2; matrix products, arithmetic and copies ran while one was open for 2% -> 0% of each run, Pallas kernels for 0% -> 0%
where the time goes in v1:
time: 423 us; the launch traced here: 422 us
  waiting for transfers between devices  292 us (69%)
  Pallas kernels  58.8 us (14%)
  starting transfers between devices  47.2 us (11%)
  between operations  13.4 us (3%)
  local copies, waits for them, and re-layouts  7.33 us (2%)
    all_gather x1, waiting for transfers between devices, body(): every = lax.all_gather(local, ('tile', 'ell'), axis_index_groups=groups)  290 us
    pallas_call x1, Pallas kernels, contract(): pl.pallas_call(contraction, out_shape=(jax.ShapeDtypeStruct((128, 4096),...  54 us
    ppermute x1, starting transfers between devices, body(): theirs = lax.ppermute(theirs, 'ell', [(0, 1), (1, 0), (2, 3), (3, 2)])  47.2 us
  transfers between devices with their start and end apart: 2, of which 2 were waited for; matrix products, arithmetic and copies ran while one was open for 0% of the time, Pallas kernels for 0%

profile of v1, /device:TPU:1, one launch (start us, length us, event | category | flops | bytes accessed | tf_op | source)
XLA Modules:
  0.0 422.2 jit_solution(12373063901703671865)
XLA Ops:
  6.5 0.0 copy-start
  6.5 0.0 all-gather.3.cloned.1.call-start
  6.5 0.8 convert_element_type.11
  7.3 0.2 copy-done
  7.5 1.2 convolution_convert_fusion
  8.8 0.6 fusion.2
  9.4 0.0 all-gather.3.cloned.1.call-update
  9.4 0.7 dynamic-slice_bitcast_fusion
  10.2 0.6 pad_add_fusion.pairs
  10.7 289.6 %all-gather.3.cloned.1.call-done = bf16[12288,128]{1,0:T(8,128)(2,1)} async-done(((bf16[192,128]{1,0:T(8,128)(2,1)}), bf16[12288,128]{1,0:T(8,128)(2,1)}) %all-gather.3.cloned.1.call-update) | async-done | bytes 3145744 | tf_op jit(solution)/shard_map/all_gather | solution.py:161
  300.4 2.3 slice.25.s_ref
  302.6 3.2 slice.24.c_ref
  305.8 54.0 %shard_map.46 = (f32[128,4096]{1,0:T(8,128)}, bf16[128,4096]{1,0:T(8,128)(2,1)}) custom-call(s32[4,128]{1,0:T(4,128)} %pad_add_fusion.pairs, bf16[64,128,128]{2,1,0:T(8,128)(2,1)} %slice.24.c_ref, bf16[64,64,128]{2,1,0:T(8,128)(2,1)} %slice.25.s_ref), custom_call_target="tpu_custom_call" | custom-call | tf_op jit(solution)/shard_map/pallas_call | solution.py:103
  359.8 47.2 %collective-permute-start = (bf16[128,4096]{1,0:T(8,128)(2,1)}, bf16[128,4096]{1,0:T(8,128)(2,1)S(1)}, u32[]{:S(2)}, u32[]{:S(2)}) collective-permute-start(bf16[128,4096]{1,0:T(8,128)(2,1)} %get-tuple-element.8), channel_id=1, source_target_pairs={{0,1},{1,0},{2,3},{3,2},{4,5},{5,4},{6,7},{7,6},{8,9},{9,8},{10,11... | collective-permute-start | bytes 3145736 | tf_op jit(solution)/shard_map/ppermute | solution.py:166
  407.0 2.5 collective-permute-done.theirs
  409.5 0.0 copy-start.1
  409.5 1.0 copy-done.1
  410.5 4.8 %shard_map.47 = f32[32,128,128]{2,1,0:T(8,128)} custom-call(f32[128,4096]{1,0:T(8,128)} %get-tuple-element.7.mine, bf16[128,4096]{1,0:T(8,128)(2,1)} %copy-done.1), custom_call_target="tpu_custom_call" | custom-call | tf_op jit(solution)/shard_map/pallas_call | solution.py:139
  (1 shorter events, 0.0 us)
Async XLA Ops:
  6.5 1.0 copy-start
  6.5 293.8 %all-gather.3.cloned.1.call-start = ((), (), s32[]{:S(2)}) async-start(), calls=%async_computation | async-start | bytes 3194880 | tf_op jit(solution)/shard_map/all_gather | solution.py:161
  359.8 49.7 %collective-permute-start = (bf16[128,4096]{1,0:T(8,128)(2,1)}, bf16[128,4096]{1,0:T(8,128)(2,1)S(1)}, u32[]{:S(2)}, u32[]{:S(2)}) collective-permute-start(bf16[128,4096]{1,0:T(8,128)(2,1)} %get-tuple-element.8), channel_id=1, source_target_pairs={{0,1},{1,0},{2,3},{3,2},{4,5},{5,4},{6,7},{7,6},{8,9},{9,8},{10,11... | collective-permute-start | bytes 3145736 | tf_op jit(solution)/shard_map/ppermute | solution.py:166
  409.5 1.0 copy-start.1
Sparse Core Ops, SparseCore 0:
  9.6 290.7 all-gather.2

commit v2 on v1

v2 whole, which is shorter than its diff:
```python
import functools
import math

import jax
import jax.numpy as jnp
from jax import lax
from jax.experimental import pallas as pl
from jax.experimental.pallas import tpu as pltpu
from jax.sharding import PartitionSpec as P

NB = 10
L = 15360
ROWS = 128
SROWS = 64
WIDE = 57
TALL = 129
GROUP = 8
BLOCKS = 64
F32 = jnp.float32
BF16 = jnp.bfloat16
MESH = pl.DeviceIdType.MESH
ORDERS = ((0, 1, 2), (1, 2, 0), (2, 0, 1))


def pair_index(first, second):
    lower = jnp.minimum(first, second)
    upper = jnp.maximum(first, second)
    return lower * NB - lower * (lower - 1) // 2 + upper - lower


def place(e):
    group = e[0] // 2 * 4 + e[1] // 2 * 2 + e[2] // 2
    return group, e[0] % 2 * 4 + e[1] % 2 * 2 + e[2] % 2


def fused(
    pairs, local, out, top, low, spec, left, right, lhs, wide, prods, acc, sent, got,
    own_sem, send_sem, recv_sem, swap_send, swap_recv,
):
    tile, ell = lax.axis_index("tile"), lax.axis_index("ell")
    half, core = ell // 2, ell % 2
    chip = (tile // 8, half * 2 + tile % 2, tile // 2 % 4)
    parts = (top, low, spec)

    def device(x, y, z, on):
        return ((x * 4 + z) * 2 + y % 2, y // 2 * 2 + on)

    def peer(axis, k):
        at = list(chip)
        at[axis] = (at[axis] + k) % 4
        return device(*at, core)

    partner = device(*chip, 1 - core)
    barrier = pltpu.get_barrier_semaphore()
    for axis in range(3):
        for k in (1, 2, 3):
            pl.semaphore_signal(barrier, inc=1, device_id=peer(axis, k), device_id_type=MESH)
    pl.semaphore_signal(barrier, inc=1, device_id=partner, device_id_type=MESH)
    pl.semaphore_wait(barrier, 10)

    def send(p, src, dst, axis, k, send_at, recv_at):
        pltpu.make_async_remote_copy(
            src_ref=src,
            dst_ref=parts[p].at[place(dst)],
            send_sem=send_sem.at[p, send_at],
            recv_sem=recv_sem.at[p, recv_at],
            device_id=peer(axis, k),
            device_id_type=MESH,
        ).start()

    def wait(p, ref, sem):
        pltpu.make_async_copy(ref, ref, sem).wait()

    for p, (d1, d2, d3) in enumerate(ORDERS):
        mine = local.at[pl.ds(64 * p, 64)]
        pltpu.make_async_copy(mine, parts[p].at[0, 0], own_sem.at[p]).start()
        for k in (1, 2, 3):
            e = [0, 0, 0]
            e[d1] = k
            send(p, mine, e, d1, k, 0, 0)
    for p, (d1, d2, d3) in enumerate(ORDERS):
        wait(p, parts[p].at[0, 0], own_sem.at[p])
        wait(p, parts[p].at[0, pl.ds(0, 3)], recv_sem.at[p, 0])
        for k in (1, 3, 2):
            for m in range(4):
                e = [0, 0, 0]
                e[d1] = m
                src = parts[p].at[place(e)]
                e[d2] = k
                send(p, src, e, d2, k, 1, 1)
    for p in range(3):
        wait(p, parts[p].at[pl.ds(0, 3), pl.ds(0, 4)], recv_sem.at[p, 1])
    for group in range(8):
        high = (group // 4, group // 2 % 2, group % 2)
        for p, (d1, d2, d3) in enumerate(ORDERS):
            for k in (1, 3, 2):
                if k // 2 != high[d3]:
                    continue
                for m in range(4):
                    e = [0, 0, 0]
                    e[d1] = 2 * high[d1] + m // 2
                    e[d2] = 2 * high[d2] + m % 2
                    src = parts[p].at[place(e)]
                    e[d3] = k
                    send(p, src, e, d3, k, 2, 2 + group)

    def arrive(group):
        high = (group // 4, group // 2 % 2, group % 2)
        for p, (d1, d2, d3) in enumerate(ORDERS):
            sem = recv_sem.at[p, 2 + group]

            @pl.when(high[d3] == 0)
            def _():
                wait(p, parts[p].at[0, pl.ds(0, 4)], sem)

            @pl.when(high[d3] == 1)
            def _():
                wait(p, parts[p].at[0], sem)

    lane = lax.broadcasted_iota(jnp.int32, (64, 128), 1)
    sublane = lax.broadcasted_iota(jnp.int32, (GROUP, 128), 0)
    lane8 = lax.broadcasted_iota(jnp.int32, (GROUP, 128), 1)
    scale = 0.5 / math.sqrt(L)

    def weights(group):
        base = jnp.zeros((GROUP, 128), jnp.int32)
        high = (group // 4, group // 2 % 2, group % 2)
        for j in range(GROUP):
            offset = (j // 4, j // 2 % 2, j % 2)
            x, y, z = ((c + 4 - 2 * h - o) % 4 for c, h, o in zip(chip, high, offset))
            at = ((x * 4 + z) * 2 + y % 2) * 4 + y // 2 * 2 + core
            base = jnp.where(sublane == j, at * 120, base)
        return (2 * (base + lane8) + 5).astype(F32) * scale

    def widen(group):
        for j in range(GROUP):
            wide[j * WIDE : j * WIDE + 56, :] = spec[group, j][:56].astype(F32)

    def product(q, weight):
        ik, jl, il, jk = (wide[pl.ds(pairs[k, q], GROUP, stride=WIDE), :] for k in range(4))
        prods[pl.ds(q, GROUP, stride=TALL), :] = weight * (ik * jl + il * jk)

    def finish(slot):
        for j in range(GROUP):
            rows = prods[j * TALL : j * TALL + 128, :]
            lhs[slot, :, j * ROWS : (j + 1) * ROWS] = rows.astype(BF16)

    def pattern(slot, group, j, i):
        for h, ref in enumerate((top, low)):
            x = ref[group, j].astype(F32)
            rows = slice(j * ROWS + 64 * h, j * ROWS + 64 * h + 64)
            if i < 8:
                at = half * 64 + (core * 32 + 8 * i) % 64 + lane // 16
                left[slot, i, rows, :] = jnp.take_along_axis(x, at, axis=1).astype(BF16)
            else:
                at = 16 * (i - 8) + lane % 16
                right[slot, i - 8, rows, :] = jnp.take_along_axis(x, at, axis=1).astype(BF16)

    every = [(j, i) for j in range(GROUP) for i in range(16)]

    acc[...] = jnp.zeros_like(acc)
    arrive(0)
    widen(0)
    first_weight = weights(0)
    lax.fori_loop(0, 128, lambda q, _: product(q, first_weight), None, unroll=8)
    finish(0)
    for j, i in every:
        pattern(0, 0, j, i)

    def two(step, _):
        for slot in range(2):
            ahead = step * 2 + slot + 1

            @pl.when(ahead < 8)
            def _():
                arrive(ahead)

            following = ahead % 8
            widen(following)
            weight = weights(following)
            for n in range(32):
                for j, i in every[4 * n : 4 * n + 4]:
                    pattern(1 - slot, following, j, i)
                for q in range(4 * n, 4 * n + 4):
                    product(q, weight)
                rhs = jnp.concatenate(
                    [left[slot, m // 8] * right[slot, m % 8] for m in (2 * n, 2 * n + 1)], axis=1
                )
                acc[:, n * 256 : (n + 1) * 256] += jnp.dot(
                    lhs[slot], rhs, preferred_element_type=F32
                )
            finish(1 - slot)

    lax.fori_loop(0, BLOCKS // GROUP // 2, two, None)

    def swap(i):
        return pltpu.make_async_remote_copy(
            src_ref=sent.at[i],
            dst_ref=got.at[i],
            send_sem=swap_send.at[i],
            recv_sem=swap_recv.at[i],
            device_id=partner,
            device_id_type=MESH,
        )

    for i in range(4):
        sent[i] = acc[:, 4096 + i * 1024 : 5120 + i * 1024].astype(BF16)
        swap(i).start()
    for p in range(3):
        wait(p, parts[p].at[0, pl.ds(0, 3)], send_sem.at[p, 0])
        wait(p, parts[p].at[pl.ds(0, 3), pl.ds(0, 4)], send_sem.at[p, 1])
        wait(p, parts[p].at[pl.ds(0, 6)], send_sem.at[p, 2])
    lane = lax.broadcasted_iota(jnp.int32, (128, 128), 1)
    for i in range(4):
        swap(i).wait()
        v = [
            acc[:, i * 1024 + j * 128 : i * 1024 + (j + 1) * 128]
            + got[i, :, j * 128 : (j + 1) * 128].astype(F32)
            for j in range(8)
        ]
        for k in (1, 2, 4):
            under = (lane // 16) & k == 0
            for m in range(8):
                if m & k == 0:
                    a, b = v[m], v[m + k]
                    v[m] = jnp.where(under, a, pltpu.roll(b, 16 * k, 1))
                    v[m + k] = jnp.where(under, pltpu.roll(a, 128 - 16 * k, 1), b)
        for m in range(8):
            out[i * 8 + m] = v[m]


def covariance(pairs, local):
    vmem = pl.BlockSpec(memory_space=pltpu.VMEM)
    return pl.pallas_call(
        fused,
        out_shape=jax.ShapeDtypeStruct((32, 128, 128), F32),
        in_specs=[pl.BlockSpec(memory_space=pltpu.SMEM), vmem],
        out_specs=vmem,
        scratch_shapes=[
            pltpu.VMEM((8, 8, 64, 128), BF16),
            pltpu.VMEM((8, 8, 64, 128), BF16),
            pltpu.VMEM((8, 8, 64, 128), BF16),
            pltpu.VMEM((2, 8, GROUP * ROWS, 128), BF16),
            pltpu.VMEM((2, 8, GROUP * ROWS, 128), BF16),
            pltpu.VMEM((2, 128, GROUP * ROWS), BF16),
            pltpu.VMEM((GROUP * WIDE, 128), F32),
            pltpu.VMEM((GROUP * TALL, 128), F32),
            pltpu.VMEM((128, 8192), F32),
            pltpu.VMEM((4, 128, 1024), BF16),
            pltpu.VMEM((4, 128, 1024), BF16),
            pltpu.SemaphoreType.DMA((3,)),
            pltpu.SemaphoreType.DMA((3, 3)),
            pltpu.SemaphoreType.DMA((3, 10)),
            pltpu.SemaphoreType.DMA((4,)),
            pltpu.SemaphoreType.DMA((4,)),
        ],
        compiler_params=pltpu.CompilerParams(
            collective_id=0, has_side_effects=True, vmem_limit_bytes=60 * 2**20
        ),
    )(pairs, local)


def body(spectra, kernel, modes, quads):
    compressed = jnp.dot(kernel, modes, preferred_element_type=F32).astype(BF16)
    local = jnp.concatenate(
        [
            jnp.pad(compressed, ((0, ROWS - 120), (0, 0))),
            jnp.pad(spectra.astype(BF16), ((0, SROWS - 55), (0, ROWS - 120))),
        ]
    )
    own = lax.dynamic_slice_in_dim(quads, lax.axis_index("tile") * 128, 128, 0).T
    i, j, k, l = own[0], own[1], own[2], own[3]
    pairs = jnp.stack([pair_index(i, k), pair_index(j, l), pair_index(i, l), pair_index(j, k)])
    return covariance(pairs, local)


def solution(mesh):
    return jax.shard_map(
        body,
        mesh=mesh,
        in_specs=(P(None, ("tile", "ell")), P(("tile", "ell"), None), P(), P()),
        out_specs=P("ell", "tile", None),
        check_vma=False,
    )
```

time: 423 us -> 65.1 us (0.15)
  waiting for transfers between devices: 292 us -> 0 us
  starting transfers between devices: 47.2 us -> 0 us
  between operations: 13.4 us -> 0.02 us
    all_gather x1 -> x0, waiting for transfers between devices: 290 us -> none  [body(): every = lax.all_gather(local, ('tile', 'ell'), axis_index_groups=groups)]
    ppermute x1 -> x0, starting transfers between devices: 47.2 us -> none  [body(): theirs = lax.ppermute(theirs, 'ell', [(0, 1), (1, 0), (2, 3), (3, 2)])]
    slice x2 -> x0, local copies, waits for them, and re-layouts: 5.45 us -> none  [body(): mine, theirs = contract(pairs, every[:, :ROWS], every[:, ROWS:])]
    pallas_call x2 -> x1, Pallas kernels: 58.8 us -> 57.7 us  [covariance(): pl.pallas_call(fused, out_shape=jax.ShapeDtypeStruct((32, 128, 128), F32)...]
  transfers between devices with their start and end apart: 2 -> 0, of which waited for: 2 -> 0; matrix products, arithmetic and copies ran while one was open for 0% -> 0% of each run, Pallas kernels for 0% -> 0%
where the time goes in v2:
time: 65.1 us; the launch traced here: 64.8 us
  Pallas kernels  57.7 us (89%)
  local copies, waits for them, and re-layouts  3.87 us (6%)
  other arithmetic  2.01 us (3%)
  matrix products  1.23 us (2%)
    pallas_call x1, Pallas kernels, covariance(): pl.pallas_call(fused, out_shape=jax.ShapeDtypeStruct((32, 128, 128), F32)...  57.7 us
    unnamed x3, local copies, waits for them, and re-layouts  3.14 us

profile of v2, /device:TPU:1, one launch (start us, length us, event | category | flops | bytes accessed | tf_op | source)
XLA Modules:
  0.0 64.8 jit_solution(2538839432172835948)
XLA Ops:
  0.0 0.0 copy-start
  0.0 0.7 %dynamic-slice_bitcast_fusion = s32[4,128]{1,0:T(4,128)S(1)} fusion(s32[4096,4]{0,1:T(4,128)} %param.7, s32[]{:T(128)S(6)} %select_n.21), kind=kLoop, calls=%fused_computation.7 | loop fusion | bytes 4100 | tf_op jit(solution)/shard_map/transpose | solution.py:271
  0.8 0.6 pad_add_fusion.pairs
  1.4 0.8 %convert_element_type.11 = bf16[55,120]{1,0:T(8,128)(2,1)S(1)} convert(f32[55,120]{1,0:T(8,128)} %param.4) | non-fusion elementwise | flops 6600 | bytes 39600 | tf_op jit(solution)/shard_map/convert_element_type | solution.py:268
  2.1 0.0 copy-done
  2.1 1.2 %convolution_convert_fusion = bf16[120,128]{1,0:T(8,128)(2,1)S(1)} fusion(bf16[120,1500]{1,0:T(8,128)(2,1)} %param.5, bf16[1500,128]{1,0:T(8,128)(2,1)S(1)} %copy-done), kind=kOutput, calls=%fused_computation | convolution fusion | flops 46095360 | bytes 774720 | tf_op jit(solution)/shard_map/dot_general | solution.py:264
  3.4 0.6 fusion.2.local
  4.0 57.7 %shard_map.46 = f32[32,128,128]{2,1,0:T(8,128)} custom-call(s32[4,128]{1,0:T(4,128)} %pad_add_fusion.pairs, bf16[192,128]{1,0:T(8,128)(2,1)} %fusion.2.local), custom_call_target="tpu_custom_call" | custom-call | tf_op jit(solution)/shard_map/pallas_call | solution.py:234
  61.7 3.1 %copy.6 = f32[32,128,128]{2,1,0:T(8,128)} copy(f32[32,128,128]{2,1,0:T(8,128)} %shard_map.46) | data formatting | bytes 4194304
  (1 shorter events, 0.0 us)
Async XLA Ops:
  0.0 2.1 %copy-start = (bf16[1500,128]{1,0:T(8,128)(2,1)S(1)}, bf16[1500,128]{1,0:T(8,128)(2,1)}, u32[]{:S(2)}) copy-start(bf16[1500,128]{1,0:T(8,128)(2,1)} %param.6) | copy-start | bytes 1152004

commit v3 on v2

--- a/solution.py
+++ b/solution.py
@@ -34,8 +34,8 @@
 
 
 def fused(
-    pairs, local, out, top, low, spec, left, right, lhs, wide, prods, acc, sent, got,
-    own_sem, send_sem, recv_sem, swap_send, swap_recv,
+    pairs, spectra, kernel, modes, out, local, top, low, spec, left, right, lhs, wide, prods, acc,
+    sent, got, own_sem, send_sem, recv_sem, swap_send, swap_recv,
 ):
     tile, ell = lax.axis_index("tile"), lax.axis_index("ell")
     half, core = ell // 2, ell % 2
@@ -56,6 +56,12 @@
         for k in (1, 2, 3):
             pl.semaphore_signal(barrier, inc=1, device_id=peer(axis, k), device_id_type=MESH)
     pl.semaphore_signal(barrier, inc=1, device_id=partner, device_id_type=MESH)
+
+    compressed = jnp.dot(kernel[...], modes[...], preferred_element_type=F32)
+    local[...] = jnp.zeros_like(local)
+    local[:120, :] = compressed.astype(BF16)
+    local[128:183, :120] = spectra[...].astype(BF16)
+    acc[...] = jnp.zeros_like(acc)
     pl.semaphore_wait(barrier, 10)
 
     def send(p, src, dst, axis, k, send_at, recv_at):
@@ -81,41 +87,67 @@
     for p, (d1, d2, d3) in enumerate(ORDERS):
         wait(p, parts[p].at[0, 0], own_sem.at[p])
         wait(p, parts[p].at[0, pl.ds(0, 3)], recv_sem.at[p, 0])
-        for k in (1, 3, 2):
-            for m in range(4):
+        for step in range(4):
+            for k, m in ((1, step), (3, 3 - step)):
                 e = [0, 0, 0]
                 e[d1] = m
                 src = parts[p].at[place(e)]
                 e[d2] = k
-                send(p, src, e, d2, k, 1, 1)
-    for p in range(3):
-        wait(p, parts[p].at[pl.ds(0, 3), pl.ds(0, 4)], recv_sem.at[p, 1])
-    for group in range(8):
-        high = (group // 4, group // 2 % 2, group % 2)
-        for p, (d1, d2, d3) in enumerate(ORDERS):
-            for k in (1, 3, 2):
-                if k // 2 != high[d3]:
-                    continue
-                for m in range(4):
-                    e = [0, 0, 0]
-                    e[d1] = 2 * high[d1] + m // 2
-                    e[d2] = 2 * high[d2] + m % 2
-                    src = parts[p].at[place(e)]
-                    e[d3] = k
-                    send(p, src, e, d3, k, 2, 2 + group)
+                on = {(1, True): 1, (3, False): 2}.get((k, m < 2), 3)
+                send(p, src, e, d2, k, 1, on)
+    for p, (d1, d2, d3) in enumerate(ORDERS):
+        for k, lines in ((1, (0, 1)), (3, (2, 3))):
+            wait(p, parts[p].at[0, pl.ds(0, 2)], recv_sem.at[p, 1 + k // 2])
+            for m in lines:
+                e = [0, 0, 0]
+                e[d1], e[d2] = m, k
+                src = parts[p].at[place(e)]
+                e[d2] = 2
+                send(p, src, e, d2, k, 1, 3)
+
+    def four(p, quarter, came, k, lands):
+        d1, d2, d3 = ORDERS[p]
+        for m in range(4):
+            e = [0, 0, 0]
+            e[d1], e[d2], e[d3] = quarter // 2 * 2 + m // 2, quarter % 2 * 2 + m % 2, came
+            src = parts[p].at[place(e)]
+            e[d3] = lands
+            send(p, src, e, d3, k, 2, 4 + 3 * quarter + lands - 1)
+
+    def landed(p, quarter, k):
+        wait(p, parts[p].at[0, pl.ds(0, 4)], recv_sem.at[p, 4 + 3 * quarter + k - 1])
+
+    def forward(p, quarter, k):
+        landed(p, quarter, k)
+        four(p, quarter, k, k, 2)
+
+    for p in range(3):
+        wait(p, parts[p].at[0], recv_sem.at[p, 3])
+        for ahead, back in ((0, 1), (3, 2)):
+            four(p, ahead, 0, 1, 1)
+            four(p, back, 0, 3, 3)
+    for p in range(3):
+        for ahead, back in ((1, 0), (2, 3)):
+            four(p, ahead, 0, 1, 1)
+            four(p, back, 0, 3, 3)
 
     def arrive(group):
         high = (group // 4, group // 2 % 2, group % 2)
         for p, (d1, d2, d3) in enumerate(ORDERS):
-            sem = recv_sem.at[p, 2 + group]
-
-            @pl.when(high[d3] == 0)
+            quarter = 2 * high[d1] + high[d2]
+            mixed = (high[d1] + high[d2]) % 2
+
+            @pl.when((1 - high[d3]) * mixed == 1)
             def _():
-                wait(p, parts[p].at[0, pl.ds(0, 4)], sem)
+                landed(p, quarter, 1)
 
             @pl.when(high[d3] == 1)
             def _():
-                wait(p, parts[p].at[0], sem)
+                landed(p, quarter, 2)
+
+            @pl.when(high[d3] * (1 - mixed) == 1)
+            def _():
+                landed(p, quarter, 3)
 
     lane = lax.broadcasted_iota(jnp.int32, (64, 128), 1)
     sublane = lax.broadcasted_iota(jnp.int32, (GROUP, 128), 0)
@@ -158,40 +190,18 @@
 
     every = [(j, i) for j in range(GROUP) for i in range(16)]
 
-    acc[...] = jnp.zeros_like(acc)
-    arrive(0)
+    for p in range(3):
+        forward(p, 0, 1)
     widen(0)
     first_weight = weights(0)
     lax.fori_loop(0, 128, lambda q, _: product(q, first_weight), None, unroll=8)
     finish(0)
     for j, i in every:
         pattern(0, 0, j, i)
-
-    def two(step, _):
-        for slot in range(2):
-            ahead = step * 2 + slot + 1
-
-            @pl.when(ahead < 8)
-            def _():
-                arrive(ahead)
-
-            following = ahead % 8
-            widen(following)
-            weight = weights(following)
-            for n in range(32):
-                for j, i in every[4 * n : 4 * n + 4]:
-                    pattern(1 - slot, following, j, i)
-                for q in range(4 * n, 4 * n + 4):
-                    product(q, weight)
-                rhs = jnp.concatenate(
-                    [left[slot, m // 8] * right[slot, m % 8] for m in (2 * n, 2 * n + 1)], axis=1
-                )
-                acc[:, n * 256 : (n + 1) * 256] += jnp.dot(
-                    lhs[slot], rhs, preferred_element_type=F32
-                )
-            finish(1 - slot)
-
-    lax.fori_loop(0, BLOCKS // GROUP // 2, two, None)
+    for p in range(3):
+        forward(p, 3, 1)
+        forward(p, 1, 3)
+        forward(p, 2, 3)
 
     def swap(i):
         return pltpu.make_async_remote_copy(
@@ -203,9 +213,42 @@
             device_id_type=MESH,
         )
 
-    for i in range(4):
-        sent[i] = acc[:, 4096 + i * 1024 : 5120 + i * 1024].astype(BF16)
-        swap(i).start()
+    def two(step, _):
+        for slot in range(2):
+            ahead = step * 2 + slot + 1
+
+            @pl.when(ahead < 8)
+            def _():
+                arrive(ahead)
+
+            following = ahead % 8
+            widen(following)
+            weight = weights(following)
+            for turn in range(32):
+                n = (turn + 16) % 32
+                for j, i in every[4 * turn : 4 * turn + 4]:
+                    pattern(1 - slot, following, j, i)
+                for q in range(4 * turn, 4 * turn + 4):
+                    product(q, weight)
+                rhs = jnp.concatenate(
+                    [left[slot, m // 8] * right[slot, m % 8] for m in (2 * n, 2 * n + 1)], axis=1
+                )
+                acc[:, n * 256 : (n + 1) * 256] += jnp.dot(
+                    lhs[slot], rhs, preferred_element_type=F32
+                )
+                if slot == 1 and turn == 15:
+
+                    @pl.when(step == 3)
+                    def _():
+                        for i in range(4):
+                            at = 4096 + i * 1024
+                            sent[i] = acc[:, at : at + 1024].astype(BF16)
+                            swap(i).start()
+
+            finish(1 - slot)
+
+    lax.fori_loop(0, BLOCKS // GROUP // 2, two, None)
+
     for p in range(3):
         wait(p, parts[p].at[0, pl.ds(0, 3)], send_sem.at[p, 0])
         wait(p, parts[p].at[pl.ds(0, 3), pl.ds(0, 4)], send_sem.at[p, 1])
@@ -229,14 +272,15 @@
             out[i * 8 + m] = v[m]
 
 
-def covariance(pairs, local):
+def covariance(pairs, spectra, kernel, modes):
     vmem = pl.BlockSpec(memory_space=pltpu.VMEM)
     return pl.pallas_call(
         fused,
         out_shape=jax.ShapeDtypeStruct((32, 128, 128), F32),
-        in_specs=[pl.BlockSpec(memory_space=pltpu.SMEM), vmem],
+        in_specs=[pl.BlockSpec(memory_space=pltpu.SMEM), vmem, vmem, vmem],
         out_specs=vmem,
         scratch_shapes=[
+            pltpu.VMEM((ROWS + SROWS, 128), BF16),
             pltpu.VMEM((8, 8, 64, 128), BF16),
             pltpu.VMEM((8, 8, 64, 128), BF16),
             pltpu.VMEM((8, 8, 64, 128), BF16),
@@ -250,28 +294,21 @@
             pltpu.VMEM((4, 128, 1024), BF16),
             pltpu.SemaphoreType.DMA((3,)),
             pltpu.SemaphoreType.DMA((3, 3)),
-            pltpu.SemaphoreType.DMA((3, 10)),
+            pltpu.SemaphoreType.DMA((3, 16)),
             pltpu.SemaphoreType.DMA((4,)),
             pltpu.SemaphoreType.DMA((4,)),
         ],
         compiler_params=pltpu.CompilerParams(
-            collective_id=0, has_side_effects=True, vmem_limit_bytes=60 * 2**20
+            collective_id=0, has_side_effects=True, vmem_limit_bytes=26 * 2**20
         ),
-    )(pairs, local)
+    )(pairs, spectra, kernel, modes)
 
 
 def body(spectra, kernel, modes, quads):
-    compressed = jnp.dot(kernel, modes, preferred_element_type=F32).astype(BF16)
-    local = jnp.concatenate(
-        [
-            jnp.pad(compressed, ((0, ROWS - 120), (0, 0))),
-            jnp.pad(spectra.astype(BF16), ((0, SROWS - 55), (0, ROWS - 120))),
-        ]
-    )
     own = lax.dynamic_slice_in_dim(quads, lax.axis_index("tile") * 128, 128, 0).T
     i, j, k, l = own[0], own[1], own[2], own[3]
     pairs = jnp.stack([pair_index(i, k), pair_index(j, l), pair_index(i, l), pair_index(j, k)])
-    return covariance(pairs, local)
+    return covariance(pairs, spectra, kernel, modes)
 
 
 def solution(mesh):

time: 65.1 us -> 61.6 us (0.946)
  other arithmetic: 2.01 us -> 0.04 us
  Pallas kernels: 57.7 us -> 56.3 us
  matrix products: 1.23 us -> 0 us
  local copies, waits for them, and re-layouts: 3.87 us -> 4.89 us
    unnamed x3 -> x9, local copies, waits for them, and re-layouts: 3.14 us -> 4.88 us
    pallas_call x1, Pallas kernels: 57.7 us -> 56.3 us  [covariance(): pl.pallas_call(fused, out_shape=jax.ShapeDtypeStruct((32, 128, 128), F32)...]
    dot_general x1 -> x0, matrix products: 1.23 us -> none  [body(): compressed = jnp.dot(kernel, modes, preferred_element_type=F32).astype(BF16)]
    convert_element_type x1 -> x0, other arithmetic: 0.75 us -> none  [body(): spectra.astype(BF16)]
    transpose x1, local copies, waits for them, and re-layouts: 0.73 us -> 0.01 us  [body(): lax.dynamic_slice_in_dim(quads, lax.axis_index('tile') * 128, 128, 0)]
where the time goes in v3:
time: 61.6 us; the launch traced here: 61.3 us
  Pallas kernels  56.3 us (91%)
  local copies, waits for them, and re-layouts  4.89 us (8%)
    pallas_call x1, Pallas kernels, covariance(): pl.pallas_call(fused, out_shape=jax.ShapeDtypeStruct((32, 128, 128), F32)...  56.3 us
    unnamed x9, local copies, waits for them, and re-layouts  4.88 us

profile of v3, /device:TPU:1, one launch (start us, length us, event | category | flops | bytes accessed | tf_op | source)
XLA Modules:
  0.0 61.3 jit_solution(10783174739518765748)
XLA Ops:
  0.0 0.0 copy-start
  0.0 0.8 %copy-done = s32[4096,4]{0,1:T(4,128)S(1)} copy-done((s32[4096,4]{0,1:T(4,128)S(1)}, s32[4096,4]{0,1:T(4,128)}, u32[]{:S(2)}) %copy-start) | copy-done | bytes 65560
  0.9 0.0 copy-start.1
  0.9 1.0 %copy-done.1 = bf16[1500,128]{1,0:T(8,128)(2,1)S(1)} copy-done((bf16[1500,128]{1,0:T(8,128)(2,1)S(1)}, bf16[1500,128]{1,0:T(8,128)(2,1)}, u32[]{:S(2)}) %copy-start.1) | copy-done | bytes 384024
  1.9 0.0 copy-start.2
  1.9 1.0 %copy-done.2 = bf16[120,1500]{1,0:T(8,128)(2,1)S(1)} copy-done((bf16[120,1500]{1,0:T(8,128)(2,1)S(1)}, bf16[120,1500]{1,0:T(8,128)(2,1)}, u32[]{:S(2)}) %copy-start.2) | copy-done | bytes 360024
  2.9 0.0 copy-start.3
  2.9 0.7 %copy-done.3 = f32[55,120]{1,0:T(8,128)S(1)} copy-done((f32[55,120]{1,0:T(8,128)S(1)}, f32[55,120]{1,0:T(8,128)}, u32[]{:S(2)}) %copy-start.3) | copy-done | bytes 26424
  3.6 56.3 %shard_map.46 = f32[32,128,128]{2,1,0:T(8,128)S(1)} custom-call(s32[4,128]{1,0:T(4,128)S(1)} %pad_add_fusion.pairs, f32[55,120]{1,0:T(8,128)S(1)} %copy-done.3, bf16[120,1500]{1,0:T(8,128)(2,1)S(1)} %copy-done.2, bf16[1500,128]{1,0:T(8,128)(2,1)S(1)} %copy-done.1), custom_call_target="tpu_custom_call" | custom-call | tf_op jit(solution)/shard_map/pallas_call | solution.py:277
  60.0 1.3 %copy.6 = f32[32,128,128]{2,1,0:T(8,128)} copy(f32[32,128,128]{2,1,0:T(8,128)S(1)} %shard_map.46) | data formatting | bytes 4194304
  (3 shorter events, 0.0 us)
Async XLA Ops:
  0.0 0.8 %copy-start = (s32[4096,4]{0,1:T(4,128)S(1)}, s32[4096,4]{0,1:T(4,128)}, u32[]{:S(2)}) copy-start(s32[4096,4]{0,1:T(4,128)} %param.7) | copy-start | bytes 196612
  0.9 1.0 %copy-start.1 = (bf16[1500,128]{1,0:T(8,128)(2,1)S(1)}, bf16[1500,128]{1,0:T(8,128)(2,1)}, u32[]{:S(2)}) copy-start(bf16[1500,128]{1,0:T(8,128)(2,1)} %modes.1) | copy-start | bytes 1152004
  1.9 1.0 %copy-start.2 = (bf16[120,1500]{1,0:T(8,128)(2,1)S(1)}, bf16[120,1500]{1,0:T(8,128)(2,1)}, u32[]{:S(2)}) copy-start(bf16[120,1500]{1,0:T(8,128)(2,1)} %kernel.1) | copy-start | bytes 1080004
  2.9 0.7 %copy-start.3 = (f32[55,120]{1,0:T(8,128)S(1)}, f32[55,120]{1,0:T(8,128)}, u32[]{:S(2)}) copy-start(f32[55,120]{1,0:T(8,128)} %spectra.1) | copy-start | bytes 79204

commit v4 on v3

--- a/solution.py
+++ b/solution.py
@@ -34,7 +34,7 @@
 
 
 def fused(
-    pairs, spectra, kernel, modes, out, local, top, low, spec, left, right, lhs, wide, prods, acc,
+    pairs, spectra_in, kernel_in, modes_in, out, spectra, kernel, modes, in_sem, local, top, low, spec, left, right, lhs, wide, prods, acc,
     sent, got, own_sem, send_sem, recv_sem, swap_send, swap_recv,
 ):
     tile, ell = lax.axis_index("tile"), lax.axis_index("ell")
@@ -51,12 +51,22 @@
         return device(*at, core)
 
     partner = device(*chip, 1 - core)
+    pulls = [
+        pltpu.make_async_copy(source, target, in_sem.at[n])
+        for n, (source, target) in enumerate(
+            ((kernel_in, kernel), (modes_in, modes), (spectra_in, spectra))
+        )
+    ]
+    for pull in pulls:
+        pull.start()
     barrier = pltpu.get_barrier_semaphore()
     for axis in range(3):
         for k in (1, 2, 3):
             pl.semaphore_signal(barrier, inc=1, device_id=peer(axis, k), device_id_type=MESH)
     pl.semaphore_signal(barrier, inc=1, device_id=partner, device_id_type=MESH)
 
+    for pull in pulls:
+        pull.wait()
     compressed = jnp.dot(kernel[...], modes[...], preferred_element_type=F32)
     local[...] = jnp.zeros_like(local)
     local[:120, :] = compressed.astype(BF16)
@@ -277,9 +287,14 @@
     return pl.pallas_call(
         fused,
         out_shape=jax.ShapeDtypeStruct((32, 128, 128), F32),
-        in_specs=[pl.BlockSpec(memory_space=pltpu.SMEM), vmem, vmem, vmem],
+        in_specs=[pl.BlockSpec(memory_space=pltpu.SMEM)]
+        + [pl.BlockSpec(memory_space=pltpu.HBM)] * 3,
         out_specs=vmem,
         scratch_shapes=[
+            pltpu.VMEM(spectra.shape, F32),
+            pltpu.VMEM(kernel.shape, BF16),
+            pltpu.VMEM(modes.shape, BF16),
+            pltpu.SemaphoreType.DMA((3,)),
             pltpu.VMEM((ROWS + SROWS, 128), BF16),
             pltpu.VMEM((8, 8, 64, 128), BF16),
             pltpu.VMEM((8, 8, 64, 128), BF16),
@@ -301,7 +316,7 @@
         compiler_params=pltpu.CompilerParams(
             collective_id=0, has_side_effects=True, vmem_limit_bytes=26 * 2**20
         ),
-    )(pairs, spectra, kernel, modes)
+    )(pairs, *(pltpu.with_memory_space_constraint(a, pltpu.HBM) for a in (spectra, kernel, modes)))
 
 
 def body(spectra, kernel, modes, quads):

time: 61.6 us -> 59.9 us (0.972)
  local copies, waits for them, and re-layouts: 4.89 us -> 2.16 us
  Pallas kernels: 56.3 us -> 57.5 us
    unnamed x9 -> x3, local copies, waits for them, and re-layouts: 4.88 us -> 2.16 us
    pallas_call x1, Pallas kernels: 56.3 us -> 57.5 us  [covariance(): pl.pallas_call(fused, out_shape=jax.ShapeDtypeStruct((32, 128, 128), F32)...]
where the time goes in v4:
time: 59.9 us; the launch traced here: 59.7 us
  Pallas kernels  57.5 us (96%)
  local copies, waits for them, and re-layouts  2.16 us (4%)
    pallas_call x1, Pallas kernels, covariance(): pl.pallas_call(fused, out_shape=jax.ShapeDtypeStruct((32, 128, 128), F32)...  57.5 us
    unnamed x3, local copies, waits for them, and re-layouts  2.16 us

profile of v4, /device:TPU:1, one launch (start us, length us, event | category | flops | bytes accessed | tf_op | source)
XLA Modules:
  0.0 59.7 jit_solution(1954969687922343247)
XLA Ops:
  0.0 0.0 copy-start
  0.0 0.8 %copy-done = s32[4096,4]{0,1:T(4,128)S(1)} copy-done((s32[4096,4]{0,1:T(4,128)S(1)}, s32[4096,4]{0,1:T(4,128)}, u32[]{:S(2)}) %copy-start) | copy-done | bytes 65560
  0.9 57.5 %shard_map.46 = f32[32,128,128]{2,1,0:T(8,128)S(1)} custom-call(s32[4,128]{1,0:T(4,128)S(1)} %pad_add_fusion.pairs, f32[55,120]{1,0:T(8,128)} %spectra_in.1, bf16[120,1500]{1,0:T(8,128)(2,1)} %kernel_in.1, bf16[1500,128]{1,0:T(8,128)(2,1)} %modes_in.1), custom_call_target="tpu_custom_call" | custom-call | tf_op jit(solution)/shard_map/pallas_call | solution.py:287
  58.4 1.3 %copy.6 = f32[32,128,128]{2,1,0:T(8,128)} copy(f32[32,128,128]{2,1,0:T(8,128)S(1)} %shard_map.46) | data formatting | bytes 4194304
  (3 shorter events, 0.0 us)
Async XLA Ops:
  0.0 0.8 %copy-start = (s32[4096,4]{0,1:T(4,128)S(1)}, s32[4096,4]{0,1:T(4,128)}, u32[]{:S(2)}) copy-start(s32[4096,4]{0,1:T(4,128)} %param.7) | copy-start | bytes 196612
